TPU v7x, 32 devices: a whole 2x2x4 slice. The times are simulated.
32 devices in a mesh: groups: 2 (over y), tok: 16 (over z, x, core).
Axes of the slice: x: 2, y: 2, z: 4, core: 2. Of those that a mesh axis runs over, the one named last changes fastest.
Arguments:
- hidden_rows: bfloat16 [4096, 3584], P(('groups', 'tok')), parts along dimension 0, may hold values from -6 to 6
- queries: bfloat16 [4096, 1792], P(('groups', 'tok')), parts along dimension 0, may hold values from -400 to 400
- labels: int32 [4096], P(('groups', 'tok')), parts along dimension 0, may hold values from 0 to 1, as said below
- doc_lengths: int32 [32], P('groups'), parts along dimension 0, may hold values from 1 to 1152, as said below
- kv_weights: bfloat16 [2, 3584, 512], replicated, may hold values from -0.09375 to 0.09375
- key_gains: float32 [2, 128], replicated, may hold values from 0.1 to 1.9
Outputs:
- attended: bfloat16 [4096, 1792], P(('groups', 'tok')), parts along dimension 0
There are 2 independent parts, one for each index of `groups`. A program takes and returns all parts, laid end to end along the dimension named above; an argument that names none is the same for every part. Nothing has to cross between parts.
Inputs may be any that keep to these rules, and one draw needn't show every extreme that they name: `labels`: 0 marks an understanding token, 1 a generation token; generation tokens come in runs. `doc_lengths`: the lengths sum to 2048; the last sample is the longest, with 1152 tokens.
All inputs are finite; a program needn't handle non-finite values.
Results may differ from a plain program's by a relative error of at most 0.0055.
The roundings to bfloat16 on the way count: a program that leaves them out, or rounds other values in their place, can miss the bound.
Values may be sent and summed in bfloat16 or wider, within the bound.
A program may use at most 128 MiB of HBM per device.

v0:
```python
import math

import jax
import jax.numpy as jnp
from jax import lax
from jax.sharding import PartitionSpec as P

HEADS = 14
KVH = 2
HD = 128


def shards(hidden_rows, queries, labels, doc_lengths, kv_weights, key_gains):
    row_count = hidden_rows.shape[0]
    device_count = lax.axis_size("tok")
    total_len = row_count * device_count
    half = KVH * HD
    groups_per = HEADS // KVH
    offset = lax.axis_index("tok") * row_count
    tower_zero = jnp.dot(hidden_rows, kv_weights[0], preferred_element_type=jnp.float32)
    tower_one = jnp.dot(hidden_rows, kv_weights[1], preferred_element_type=jnp.float32)
    chosen = labels[:, None] == 1
    projected = jnp.where(chosen, tower_one, tower_zero)
    keys = projected[:, :half].reshape(row_count, KVH, HD)
    square_mean = jnp.mean(keys * keys, axis=-1, keepdims=True)
    gains = jnp.where(chosen, key_gains[1][None, :], key_gains[0][None, :])
    keys = (keys * lax.rsqrt(square_mean + 1e-06) * gains[:, None, :]).astype(jnp.bfloat16)
    values = projected[:, half:].astype(jnp.bfloat16)
    packed = jnp.concatenate([keys.reshape(row_count, half), values], axis=1)
    positions = offset + jnp.arange(row_count, dtype=jnp.int32)
    ends = jnp.cumsum(doc_lengths)
    first_pos = jnp.max(jnp.where(ends[None, :] <= positions[:, None], ends[None, :], 0), axis=1)
    last_pos = (
        jnp.min(jnp.where(ends[None, :] > positions[:, None], ends[None, :], total_len), axis=1) - 1
    )
    local_zero = jnp.where(labels == 0, positions, total_len)
    suffix = lax.cummin(local_zero, axis=0, reverse=True)
    earliest = jnp.min(local_zero)
    every = lax.all_gather(earliest.reshape(1), "tok", axis=0, tiled=True)
    device_ids = jnp.arange(device_count, dtype=jnp.int32)
    later = jnp.min(jnp.where(device_ids > lax.axis_index("tok"), every, total_len))
    zero_next = jnp.minimum(suffix, later)
    reach = jnp.where(labels == 1, jnp.minimum(last_pos, zero_next - 1), positions)
    lowest = jnp.min(first_pos)
    highest = jnp.max(reach)
    query_rows = queries.reshape(row_count, KVH, groups_per, HD)
    scale = 1.0 / HD**0.5

    def update(carry, block_rows, key_pos):
        peak, summed, accum = carry
        block_keys = block_rows[:, :half].reshape(-1, KVH, HD)
        block_values = block_rows[:, half:].reshape(-1, KVH, HD)
        visible = (key_pos[None, :] >= first_pos[:, None]) & (key_pos[None, :] <= reach[:, None])
        visible = visible[:, None, None, :]
        scores = (
            jnp.einsum("tkgd,skd->tkgs", query_rows, block_keys, preferred_element_type=jnp.float32)
            * scale
        )
        scores = jnp.where(visible, scores, -1e30)
        new_peak = jnp.maximum(peak, jnp.max(scores, axis=-1))
        weight = jnp.where(visible, jnp.exp(scores - new_peak[..., None]), 0.0)
        factor = jnp.exp(peak - new_peak)
        summed = summed * factor + jnp.sum(weight, axis=-1)
        mixed = jnp.einsum(
            "tkgs,skd->tkgd",
            weight.astype(jnp.bfloat16),
            block_values,
            preferred_element_type=jnp.float32,
        )
        accum = accum * factor[..., None] + mixed
        return (new_peak, summed, accum)

    start_state = (
        jnp.full((row_count, KVH, groups_per), -1e30, jnp.float32),
        jnp.zeros((row_count, KVH, groups_per), jnp.float32),
        jnp.zeros((row_count, KVH, groups_per, HD), jnp.float32),
    )
    piece = lax.all_gather(packed, "tok", axis=0, tiled=True)
    piece_rows = piece.shape[0]
    block = math.gcd(piece_rows, 512)

    def step(block_index, state):
        block_rows = lax.dynamic_slice_in_dim(piece, block_index * block, block, 0)
        key_pos = block_index * block + jnp.arange(block, dtype=jnp.int32)
        needed = (key_pos[0] <= highest) & (key_pos[block - 1] >= lowest)
        return lax.cond(
            needed, lambda inner: update(inner, block_rows, key_pos), lambda inner: inner, state
        )

    final_state = lax.fori_loop(0, piece_rows // block, step, start_state)
    result = final_state[2] / final_state[1][..., None]
    return result.reshape(row_count, HEADS * HD).astype(jnp.bfloat16)


def solution(mesh):
    in_specs = (
        P(("groups", "tok"), None),
        P(("groups", "tok"), None),
        P(("groups", "tok")),
        P("groups"),
        P(),
        P(),
    )
    out_specs = P(("groups", "tok"), None)
    return jax.shard_map(shards, mesh=mesh, in_specs=in_specs, out_specs=out_specs, check_vma=False)
```

profile of v0, /device:TPU:24, one launch (start us, length us, event | category | flops | bytes accessed | tf_op | source)
XLA Modules:
  0.0 95.2 jit_solution(1849011309548672089)
XLA Ops:
  6.5 0.7 broadcast_compare_fusion
  7.7 2.7 %fusion.15 = f32[128,512]{1,0:T(8,128)S(1)} fusion(bf16[128,3584]{1,0:T(8,128)(2,1)S(1)} %copy-done, bf16[2,3584,512]{2,1,0:T(8,128)(2,1)} %param.14), kind=kOutput, calls=%fused_computation.17 | convolution fusion | flops 469762048 | bytes 4849664 | tf_op jit(solution)/shard_map/dot_general | solution.py:20
  10.5 2.7 %fusion.21 = f32[128,512]{1,0:T(8,128)S(1)} fusion(f32[128,512]{1,0:T(8,128)S(1)} %fusion.15, bf16[128,3584]{1,0:T(8,128)(2,1)S(1)} %copy-done, bf16[2,3584,512]{2,1,0:T(8,128)(2,1)} %param.14, pred[128]{0:T(512)(128)(4,1)S(1)} %broadcast_compare_fusion), kind=kOutput, calls=%fused_computation.23 | convolution fusion | flops 469827584 | bytes 5111936 | tf_op jit(solution)/shard_map/dot_general | solution.py:21
  14.0 0.7 pad_maximum_fusion
  15.9 1.3 %dynamic-update-slice = s32[16]{0:T(128)S(1)} dynamic-update-slice(s32[16]{0:T(128)S(1)} %broadcast.97, s32[1]{0:T(128)} %bitcast.10, u32[]{:T(128)} %bitcast.11) | dynamic-update-slice | bytes 12
  17.3 8.9 %all-reduce = s32[16]{0:T(128)S(1)} all-reduce(s32[16]{0:T(128)S(1)} %dynamic-update-slice), channel_id=1, replica_groups=mesh['groups'=2,'tok'=16] {'tok'}, use_global_device_ids=true, to_apply=%add | all-reduce | flops 16 | bytes 128
  26.6 0.6 reduce_min.39
  27.3 2.2 %reduce-window.18 = s32[128,1]{1,0:T(8,128)S(1)} reduce-window(s32[128,1]{1,0:T(8,128)S(1)} %copy.46, s32[]{:T(128)} %constant.86.clone.1), window={size=128x1 pad=0_127x0_0}, to_apply=%region_3.4 | reduce-window | flops 16256 | bytes 1028 | tf_op jit(solution)/shard_map/reduce-window.8
  30.0 0.7 fusion.25
  30.7 0.7 add_reduce_fusion
  31.4 0.7 fusion.28
  32.1 23.9 %all-gather.2.cloned.1.call-done = bf16[2048,512]{1,0:T(8,128)(2,1)} async-done(((bf16[128,512]{1,0:T(8,128)(2,1)}), bf16[2048,512]{1,0:T(8,128)(2,1)}) %all-gather.2.cloned.1.call-update) | async-done | bytes 2097168 | tf_op jit(solution)/shard_map/all_gather | solution.py:78
  56.0 2.9 %copy.50 = bf16[2048,512]{0,1:T(8,128)(2,1)S(1)} copy(bf16[2048,512]{1,0:T(8,128)(2,1)} %all-gather.2.cloned.1.call-done) | data formatting | bytes 4194304 | tf_op jit(solution)/shard_map/while | solution.py:90
  59.0 1.0 %broadcast_in_dim.113 = f32[128,2,7,128]{3,0,2,1:T(8,128)} broadcast(f32[]{:T(128)} %constant.79.clone.1), dimensions={} | broadcast | bytes 917508 | tf_op jit(solution)/shard_map/broadcast_in_dim | solution.py:76
  60.0 25.8 %while.17 = (s32[]{:T(128)}, f32[128,2,7]{0,2,1:T(8,128)S(1)}, f32[128,2,7]{0,2,1:T(8,128)S(1)}, f32[128,2,7,128]{3,0,2,1:T(8,128)}, s32[]{:T(128)}, /*index=5*/...) while((s32[]{:T(128)}, f32[128,2,7]{0,2,1:T(8,128)S(1)}, ...), condition=%wide.region_14.15_spmd, body=%wide.region_9.14_spmd.sunk | while | flops 482349056 | bytes 22599068 | solution.py:90
  66.3 4.4 %conditional.2 = ((f32[128,2,7]{0,2,1:T(8,128)S(1)}, f32[128,2,7]{0,2,1:T(8,128)S(1)}, f32[128,2,7,128]{3,0,2,1:T(8,128)})) conditional(s32[]{:T(128)} %convert_element_type.35, (f32[128,2,7]{0,2,1:T(8,128)S(1)}, f32[128,2,7]{0,2,1:T(8,128)S(1)}, f32[128,2,7,128]{3,0,2,1:T(8,128)}) %tuple.58, (s32[512]{0:T(512)S(1)}, s32[128]{0:T(128)S(1)}, ...), branch_computations={%region_10.10_spmd, %region_11.13_spmd} | conditional | flops 482348544 | bytes 22596750 | solution.py:86
  66.5 0.8 fusion
  67.3 0.9 fusion.2
  68.2 1.5 %fusion.9 = f32[128,2,7,128]{3,0,2,1:T(8,128)S(1)} fusion(bf16[512,2,128,1]{0,2,3,1:T(8,128)(2,1)S(1)} %bitcast.70, f32[2,512,128,7]{2,1,3,0:T(8,128)S(1)} %get-tuple-element.344, f32[128,2,7]{0,2,1:T(8,128)S(1)} %max.4, pred[128,512]{0,1:T(8,128)(4,1)S(1)} %compare_and_fusion, f32[128,2,7,128]{3,0,2,1:T(8,128)S(1)} %copy-done.1, ...), kind=kOutput, calls=%fused_computation.8 | convolution fusion | flops 239927296 | bytes 5847040 | tf_op jit(solution)/shard_map/while/body/eval_jaxpr/cond/branch_1_fun/tkgs,skd->tkgd/dot_general | solution.py:64
  69.8 0.9 copy-done.2
  73.8 4.4 %conditional.2 = ((f32[128,2,7]{0,2,1:T(8,128)S(1)}, f32[128,2,7]{0,2,1:T(8,128)S(1)}, f32[128,2,7,128]{3,0,2,1:T(8,128)})) conditional(s32[]{:T(128)} %convert_element_type.35, (f32[128,2,7]{0,2,1:T(8,128)S(1)}, f32[128,2,7]{0,2,1:T(8,128)S(1)}, f32[128,2,7,128]{3,0,2,1:T(8,128)}) %tuple.58, (s32[512]{0:T(512)S(1)}, s32[128]{0:T(128)S(1)}, ...), branch_computations={%region_10.10_spmd, %region_11.13_spmd} | conditional | flops 482348544 | bytes 22596750 | solution.py:86
  74.0 0.8 fusion
  74.8 0.9 fusion.2
  75.8 1.5 %fusion.9 = f32[128,2,7,128]{3,0,2,1:T(8,128)S(1)} fusion(bf16[512,2,128,1]{0,2,3,1:T(8,128)(2,1)S(1)} %bitcast.70, f32[2,512,128,7]{2,1,3,0:T(8,128)S(1)} %get-tuple-element.344, f32[128,2,7]{0,2,1:T(8,128)S(1)} %max.4, pred[128,512]{0,1:T(8,128)(4,1)S(1)} %compare_and_fusion, f32[128,2,7,128]{3,0,2,1:T(8,128)S(1)} %copy-done.1, ...), kind=kOutput, calls=%fused_computation.8 | convolution fusion | flops 239927296 | bytes 5847040 | tf_op jit(solution)/shard_map/while/body/eval_jaxpr/cond/branch_1_fun/tkgs,skd->tkgd/dot_general | solution.py:64
  77.3 0.9 copy-done.2
  81.4 4.4 %conditional.2 = ((f32[128,2,7]{0,2,1:T(8,128)S(1)}, f32[128,2,7]{0,2,1:T(8,128)S(1)}, f32[128,2,7,128]{3,0,2,1:T(8,128)})) conditional(s32[]{:T(128)} %convert_element_type.35, (f32[128,2,7]{0,2,1:T(8,128)S(1)}, f32[128,2,7]{0,2,1:T(8,128)S(1)}, f32[128,2,7,128]{3,0,2,1:T(8,128)}) %tuple.58, (s32[512]{0:T(512)S(1)}, s32[128]{0:T(128)S(1)}, ...), branch_computations={%region_10.10_spmd, %region_11.13_spmd} | conditional | flops 482348544 | bytes 22596750 | solution.py:86
  81.6 0.8 fusion
  82.4 0.9 fusion.2
  83.3 1.5 %fusion.9 = f32[128,2,7,128]{3,0,2,1:T(8,128)S(1)} fusion(bf16[512,2,128,1]{0,2,3,1:T(8,128)(2,1)S(1)} %bitcast.70, f32[2,512,128,7]{2,1,3,0:T(8,128)S(1)} %get-tuple-element.344, f32[128,2,7]{0,2,1:T(8,128)S(1)} %max.4, pred[128,512]{0,1:T(8,128)(4,1)S(1)} %compare_and_fusion, f32[128,2,7,128]{3,0,2,1:T(8,128)S(1)} %copy-done.1, ...), kind=kOutput, calls=%fused_computation.8 | convolution fusion | flops 239927296 | bytes 5847040 | tf_op jit(solution)/shard_map/while/body/eval_jaxpr/cond/branch_1_fun/tkgs,skd->tkgd/dot_general | solution.py:64
  84.8 0.9 copy-done.2
  85.8 1.5 %copy.52 = f32[128,2,7,128]{0,3,2,1:T(8,128)S(1)} copy(f32[128,2,7,128]{3,0,2,1:T(8,128)} %get-tuple-element.273) | data formatting | bytes 1835008 | tf_op jit(solution)/shard_map/while | solution.py:90
  87.4 1.0 %copy.53 = bf16[128,1792]{1,0:T(8,128)(2,1)} copy(bf16[128,1792]{0,1:T(8,128)(2,1)S(1)} %bitcast.72) | data formatting | bytes 917504 | tf_op jit(solution)/shard_map/convert_element_type | solution.py:92
  (70 shorter events, 6.6 us)
Async XLA Ops:
  6.5 1.2 %copy-start = (bf16[128,3584]{1,0:T(8,128)(2,1)S(1)}, bf16[128,3584]{1,0:T(8,128)(2,1)}, u32[]{:S(2)}) copy-start(bf16[128,3584]{1,0:T(8,128)(2,1)} %param.10) | copy-start | bytes 2752516
  6.5 49.5 %all-gather.2.cloned.1.call-start = ((), (), s32[]{:S(2)}) async-start(), calls=%async_computation | async-start | bytes 2228224 | tf_op jit(solution)/shard_map/all_gather | solution.py:78
  10.4 2.8 %copy-start.5 = (f32[2,128]{1,0:T(2,128)S(1)}, f32[2,128]{1,0:T(2,128)}, u32[]{:S(2)}) copy-start(f32[2,128]{1,0:T(2,128)} %param.15) | copy-start | bytes 3076
  10.4 4.2 %copy-start.7 = (u32[32]{0:T(128)S(1)}, u32[32]{0:T(128)}, u32[]{:S(2)}) copy-start(u32[32]{0:T(128)} %constant.91) | copy-start | bytes 388
  10.4 4.9 %copy-start.4 = (s32[128]{0:T(128)S(1)}, s32[128]{0:T(128)}, u32[]{:S(2)}) copy-start(s32[128]{0:T(128)} %param.12) | copy-start | bytes 1540
  10.4 15.7 %copy-start.6 = (s32[16]{0:T(128)S(1)}, s32[16]{0:T(128)}, u32[]{:S(2)}) copy-start(s32[16]{0:T(128)} %param.13) | copy-start | bytes 196
  10.5 19.0 %copy-start.3 = (bf16[128,1792]{1,0:T(8,128)(2,1)S(1)}, bf16[128,1792]{1,0:T(8,128)(2,1)}, u32[]{:S(2)}) copy-start(bf16[128,1792]{1,0:T(8,128)(2,1)} %param.11) | copy-start | bytes 1376260
  66.5 1.7 %copy-start.1 = (f32[128,2,7,128]{3,0,2,1:T(8,128)S(1)}, f32[128,2,7,128]{3,0,2,1:T(8,128)}, u32[]{:S(2)}) copy-start(f32[128,2,7,128]{3,0,2,1:T(8,128)} %get-tuple-element.256) | copy-start | bytes 2752516 | tf_op jit(solution)/shard_map/while/body/eval_jaxpr/cond
  69.8 0.9 copy-start.2
  74.0 1.7 %copy-start.1 = (f32[128,2,7,128]{3,0,2,1:T(8,128)S(1)}, f32[128,2,7,128]{3,0,2,1:T(8,128)}, u32[]{:S(2)}) copy-start(f32[128,2,7,128]{3,0,2,1:T(8,128)} %get-tuple-element.256) | copy-start | bytes 2752516 | tf_op jit(solution)/shard_map/while/body/eval_jaxpr/cond
  77.3 0.9 copy-start.2
  81.6 1.7 %copy-start.1 = (f32[128,2,7,128]{3,0,2,1:T(8,128)S(1)}, f32[128,2,7,128]{3,0,2,1:T(8,128)}, u32[]{:S(2)}) copy-start(f32[128,2,7,128]{3,0,2,1:T(8,128)} %get-tuple-element.256) | copy-start | bytes 2752516 | tf_op jit(solution)/shard_map/while/body/eval_jaxpr/cond
  84.8 0.9 copy-start.2
Sparse Core Ops, SparseCore 0:
  14.8 41.1 all-gather.1
where the time goes:
time: 96 us; the launch traced here: 95.2 us
  waiting for transfers between devices  23.9 us (25%)
  local copies, waits for them, and re-layouts  15.3 us (16%)
  between operations  13.6 us (14%)
  matrix products  12.3 us (13%)
  other arithmetic  10.8 us (11%)
  loops' own time  10.4 us (11%)
  blocking collectives  8.91 us (9%)
    all_gather x1, waiting for transfers between devices, shards(): piece = lax.all_gather(packed, 'tok', axis=0, tiled=True)  23.9 us
    another operation x1, loops' own time, shards(): final_state = lax.fori_loop(0, piece_rows // block, step, start_state)  10.1 us
    unnamed x1, blocking collectives  8.91 us
    while x3, local copies, waits for them, and re-layouts, shards(): final_state = lax.fori_loop(0, piece_rows // block, step, start_state)  4.67 us
    dot_general x3, matrix products, update(): jnp.einsum('tkgs,skd->tkgd', weight.astype(jnp.bfloat16), block_values, p...  4.57 us
    cond x15, local copies, waits for them, and re-layouts  2.79 us
    dot_general x1, matrix products, shards(): jnp.dot(hidden_rows, kv_weights[1], preferred_element_type=jnp.float32)  2.73 us
    unnamed x16, local copies, waits for them, and re-layouts  2.7 us
  transfers between devices with their start and end apart: 1, of which 1 were waited for; matrix products, arithmetic and copies ran while one was open for 9% of the time, Pallas kernels for 0%

commit v1 on v0

v1 whole, which is shorter than its diff:
```python
import functools
import math

import jax
import jax.numpy as jnp
from jax import lax
from jax.experimental import pallas as pl
from jax.experimental.pallas import tpu as pltpu
from jax.sharding import PartitionSpec as P

HEADS = 14
KVH = 2
HD = 128
GROUPS_PER = HEADS // KVH
HALF = KVH * HD
MESH = pl.DeviceIdType.MESH
NEG = -1e30


def kernel(
    n,
    chunk,
    labels_ref,
    lengths_ref,
    gains_ref,
    hidden_hbm,
    queries_hbm,
    weights_hbm,
    out_ref,
    hidden,
    query,
    weights,
    held,
    zeros_at,
    peak,
    summed,
    accum,
    in_sem,
    query_sem,
    weight_sem,
    send_sem,
    recv_sem,
    pass_sem,
    zsend_sem,
    zrecv_sem,
):
    rows, depth = hidden.shape
    total_len = n * rows
    me = lax.axis_index("tok")
    core = lax.rem(me, 2)
    partner = me + 1 - 2 * core
    split = n // 2 - 1
    upper = me >= split
    low = jnp.where(upper, split, 0)
    high = jnp.where(upper, n, split)
    paired = (partner >= low) & (partner < high)
    lone = jnp.where(upper, split, split - 1)
    unused = jnp.where(upper, split - 1, split)

    def block(j):
        return pl.ds(pl.multiple_of(j * rows, rows), rows)

    hidden_copy = pltpu.make_async_copy(hidden_hbm, hidden, in_sem)
    hidden_copy.start()
    chunks = depth // chunk
    weight_copies = []
    for i in range(chunks):
        part = pl.ds(i * chunk, chunk)
        copy = pltpu.make_async_copy(
            weights_hbm.at[:, part, :], weights.at[:, part, :], weight_sem.at[i]
        )
        copy.start()
        weight_copies.append(copy)
    query_copies = []
    for h in range(HEADS):
        copy = pltpu.make_async_copy(
            queries_hbm.at[:, pl.ds(h * HD, HD)],
            query.at[pl.ds(h * rows, rows), :],
            query_sem.at[h],
        )
        copy.start()
        query_copies.append(copy)

    offset = me * rows
    lane_pos = offset + lax.broadcasted_iota(jnp.int32, (1, rows), 1)
    labels = labels_ref[...]
    first_lane = jnp.zeros((1, rows), jnp.int32)
    last_lane = jnp.full((1, rows), total_len, jnp.int32)
    end = jnp.int32(0)
    for i in range(lengths_ref.shape[0]):
        end = end + lengths_ref[i]
        first_lane = jnp.maximum(first_lane, jnp.where(end <= lane_pos, end, 0))
        last_lane = jnp.minimum(last_lane, jnp.where(end > lane_pos, end, total_len))
    last_lane = last_lane - 1
    row_at = lax.broadcasted_iota(jnp.int32, (rows, rows), 0)
    lane_at = lax.broadcasted_iota(jnp.int32, (rows, rows), 1)
    diagonal = row_at == lane_at

    def to_rows(lane_values):
        spread = jnp.where(diagonal, jnp.broadcast_to(lane_values, (rows, rows)), 0)
        return jnp.sum(spread, axis=1, keepdims=True)

    first = to_rows(first_lane)
    last = to_rows(last_lane)
    label = to_rows(labels)
    zero_lane = jnp.where(labels == 0, lane_pos, total_len)
    local_zero = jnp.min(
        jnp.where(lane_at >= row_at, jnp.broadcast_to(zero_lane, (rows, rows)), total_len),
        axis=1,
        keepdims=True,
    )
    earliest = jnp.min(zero_lane, axis=1, keepdims=True)
    zeros_at[...] = jnp.full(zeros_at.shape, total_len, jnp.int32)
    zeros_at[me] = jnp.broadcast_to(earliest, (8, rows))
    held[block(unused), :] = jnp.zeros((rows, 2 * HALF), jnp.bfloat16)
    peak[...] = jnp.full(peak.shape, NEG, jnp.float32)
    summed[...] = jnp.zeros(summed.shape, jnp.float32)
    accum[...] = jnp.zeros(accum.shape, jnp.float32)

    barrier = pltpu.get_barrier_semaphore()

    @pl.loop(low, high)
    def _(d):
        @pl.when(d != me)
        def _():
            pl.semaphore_signal(barrier, inc=1, device_id={"tok": d}, device_id_type=MESH)

    def zero_copy(source, target):
        return pltpu.make_async_remote_copy(
            src_ref=zeros_at.at[source],
            dst_ref=zeros_at.at[source],
            send_sem=zsend_sem.at[target],
            recv_sem=zrecv_sem.at[source],
            device_id={"tok": target},
            device_id_type=MESH,
        )

    def own_copy(source, target):
        return pltpu.make_async_remote_copy(
            src_ref=held.at[block(source), :],
            dst_ref=held.at[block(source), :],
            send_sem=send_sem.at[target],
            recv_sem=recv_sem.at[source],
            device_id={"tok": target},
            device_id_type=MESH,
        )

    def pass_copy(source):
        return pltpu.make_async_remote_copy(
            src_ref=held.at[block(source), :],
            dst_ref=held.at[block(source), :],
            send_sem=pass_sem.at[source],
            recv_sem=recv_sem.at[source],
            device_id={"tok": partner},
            device_id_type=MESH,
        )

    hidden_copy.wait()
    projected = [jnp.zeros((rows, 2 * HALF), jnp.float32) for _ in range(2)]
    for i in range(chunks):
        weight_copies[i].wait()
        part = pl.ds(i * chunk, chunk)
        for tower in range(2):
            projected[tower] = projected[tower] + jnp.dot(
                hidden[:, part], weights[tower, part, :], preferred_element_type=jnp.float32
            )
        if i == chunks // 2:
            pl.semaphore_wait(barrier, high - low - 1)

            @pl.loop(low, me)
            def _(d):
                zero_copy(me, d).start()

    chosen = label == 1
    gains = jnp.where(chosen, gains_ref[1:2, :], gains_ref[0:1, :])
    mine = jnp.where(chosen, projected[1], projected[0])
    for g in range(KVH):
        key = mine[:, g * HD : (g + 1) * HD]
        square_mean = jnp.mean(key * key, axis=-1, keepdims=True)
        key = key * lax.rsqrt(square_mean + 1e-06) * gains
        held[block(me), g * HD : (g + 1) * HD] = key.astype(jnp.bfloat16)
    held[block(me), HALF:] = mine[:, HALF:].astype(jnp.bfloat16)

    def own_target(d):
        same = lax.rem(d, 2) == core
        return (d != me) & (same | (d == partner) | (d == lone))

    count = high - low

    @pl.loop(1, count)
    def _(k):
        d = low + lax.rem(me - low - k + count, count)

        @pl.when(own_target(d))
        def _():
            own_copy(me, d).start()

    @pl.loop(me + 1, high)
    def _(d):
        zero_copy(d, me).wait_recv()

    device_at = lax.broadcasted_iota(jnp.int32, zeros_at.shape, 0)
    later = jnp.min(jnp.where(device_at > me, zeros_at[...], total_len), axis=0)
    later = later[0:1, 0:1]
    zero_next = jnp.minimum(local_zero, later)
    row_pos = offset + lax.broadcasted_iota(jnp.int32, (rows, 1), 0)
    reach = jnp.where(label == 1, jnp.minimum(last, zero_next - 1), row_pos)
    for copy in query_copies:
        copy.wait()

    factor_of = (1.0 / HD**0.5) * math.log2(math.e)
    chip_low = low // 2
    chip_count = (high + 1) // 2 - chip_low
    my_chip = me // 2
    pair = 2 * rows

    @pl.loop(0, chip_count)
    def _(t):
        chip = chip_low + lax.rem(my_chip - chip_low + t, chip_count)
        same = 2 * chip + core
        other = 2 * chip + 1 - core

        @pl.when((same != me) & (same >= low) & (same < high))
        def _():
            own_copy(same, me).wait_recv()

            @pl.when(paired)
            def _():
                pass_copy(same).start()

        @pl.when((other >= low) & (other < high))
        def _():
            own_copy(other, me).wait_recv()

        start = pl.multiple_of(chip * pair, pair)
        key_pos = start + lax.broadcasted_iota(jnp.int32, (rows, pair), 1)
        bias = jnp.where((key_pos >= first) & (key_pos <= reach), 0.0, NEG)
        for g in range(KVH):
            group = pl.ds(g * GROUPS_PER * rows, GROUPS_PER * rows)
            keys = held[pl.ds(start, pair), g * HD : (g + 1) * HD]
            values = held[pl.ds(start, pair), HALF + g * HD : HALF + (g + 1) * HD]
            scores = lax.dot_general(
                query[group, :],
                keys,
                (((1,), (1,)), ((), ())),
                preferred_element_type=jnp.float32,
            )
            scores = scores.reshape(GROUPS_PER, rows, pair)
            scores = jnp.where(bias[None] == 0.0, scores, NEG)
            scores = scores.reshape(GROUPS_PER * rows, pair)
            old_peak = peak[group, :]
            new_peak = jnp.maximum(old_peak, jnp.max(scores, axis=-1, keepdims=True))
            weight = jnp.exp2((scores - new_peak) * factor_of)
            factor = jnp.exp2((old_peak - new_peak) * factor_of)
            peak[group, :] = new_peak
            summed[group, :] = summed[group, :] * factor + jnp.sum(weight, axis=-1, keepdims=True)
            mixed = jnp.dot(
                weight.astype(jnp.bfloat16), values, preferred_element_type=jnp.float32
            )
            accum[group, :] = accum[group, :] * factor + mixed

    for h in range(HEADS):
        head = pl.ds(h * rows, rows)
        result = accum[head, :] / summed[head, :]
        out_ref[:, h * HD : (h + 1) * HD] = result.astype(out_ref.dtype)

    @pl.loop(low, me)
    def _(d):
        zero_copy(me, d).wait_send()

    @pl.loop(low, high)
    def _(d):
        @pl.when(own_target(d))
        def _():
            own_copy(me, d).wait_send()

        @pl.when(paired & (d != me) & (lax.rem(d, 2) == core))
        def _():
            pass_copy(d).wait_send()


def solution(mesh):
    n = mesh.shape["tok"]

    def shards(hidden_rows, queries, labels, doc_lengths, kv_weights, key_gains):
        rows, depth = hidden_rows.shape
        chunk = math.gcd(depth, 512)
        any_space = pl.BlockSpec(memory_space=pl.ANY)
        vmem = pl.BlockSpec(memory_space=pltpu.VMEM)
        return pl.pallas_call(
            functools.partial(kernel, n, chunk),
            out_shape=jax.ShapeDtypeStruct(queries.shape, jnp.bfloat16),
            in_specs=[
                vmem,
                pl.BlockSpec(memory_space=pltpu.SMEM),
                vmem,
                any_space,
                any_space,
                any_space,
            ],
            out_specs=vmem,
            scratch_shapes=[
                pltpu.VMEM((rows, depth), jnp.bfloat16),
                pltpu.VMEM((HEADS * rows, HD), jnp.bfloat16),
                pltpu.VMEM(kv_weights.shape, jnp.bfloat16),
                pltpu.VMEM((n * rows, 2 * HALF), jnp.bfloat16),
                pltpu.VMEM((n, 8, rows), jnp.int32),
                pltpu.VMEM((HEADS * rows, 1), jnp.float32),
                pltpu.VMEM((HEADS * rows, 1), jnp.float32),
                pltpu.VMEM((HEADS * rows, HD), jnp.float32),
                pltpu.SemaphoreType.DMA,
                pltpu.SemaphoreType.DMA((HEADS,)),
                pltpu.SemaphoreType.DMA((depth // chunk,)),
                pltpu.SemaphoreType.DMA((n,)),
                pltpu.SemaphoreType.DMA((n,)),
                pltpu.SemaphoreType.DMA((n,)),
                pltpu.SemaphoreType.DMA((n,)),
                pltpu.SemaphoreType.DMA((n,)),
            ],
            compiler_params=pltpu.CompilerParams(collective_id=0, has_side_effects=True),
        )(labels.reshape(1, rows), doc_lengths, key_gains, hidden_rows, queries, kv_weights)

    in_specs = (
        P(("groups", "tok"), None),
        P(("groups", "tok"), None),
        P(("groups", "tok")),
        P("groups"),
        P(),
        P(),
    )
    out_specs = P(("groups", "tok"), None)
    return jax.shard_map(shards, mesh=mesh, in_specs=in_specs, out_specs=out_specs, check_vma=False)
```

time: 96 us -> 31.2 us (0.33)
  Pallas kernels: 0 us -> 29.3 us
  waiting for transfers between devices: 23.9 us -> 0 us
  between operations: 13.6 us -> 0.01 us
  local copies, waits for them, and re-layouts: 15.3 us -> 1.82 us
  matrix products: 12.3 us -> 0 us
  other arithmetic: 10.8 us -> 0 us
  loops' own time: 10.4 us -> 0 us
  blocking collectives: 8.91 us -> 0 us
    pallas_call x0 -> x1, Pallas kernels: none -> 29.3 us  [shards(): pl.pallas_call(functools.partial(kernel, n, chunk), out_shape=jax.ShapeDt...]
    all_gather x1 -> x0, waiting for transfers between devices: 23.9 us -> none  [shards(): piece = lax.all_gather(packed, 'tok', axis=0, tiled=True)]
    dot_general x8 -> x0, matrix products: 12.3 us -> none  [the longest x3 4.57 us: update(): jnp.einsum('tkgs,skd->tkgd', weight.astype(jnp.bfloat16), block_values, p...]
    another operation x5 -> x0, loops' own time: 10.4 us -> none  [the longest x1 10.1 us: shards(): final_state = lax.fori_loop(0, piece_rows // block, step, start_state)]
    unnamed x1 -> x0, blocking collectives: 8.91 us -> none
    while x3 -> x0, local copies, waits for them, and re-layouts: 4.67 us -> none  [shards(): final_state = lax.fori_loop(0, piece_rows // block, step, start_state)]
    reduce_sum x4 -> x0, other arithmetic: 2.86 us -> none  [the longest x3 2.66 us: update(): summed = summed * factor + jnp.sum(weight, axis=-1)]
    cond x15 -> x0, local copies, waits for them, and re-layouts: 2.79 us -> none
  transfers between devices with their start and end apart: 1 -> 0, of which waited for: 1 -> 0; matrix products, arithmetic and copies ran while one was open for 9% -> 0% of each run, Pallas kernels for 0% -> 0%
where the time goes in v1:
time: 31.2 us; the launch traced here: 31.1 us
  Pallas kernels  29.3 us (94%)
  local copies, waits for them, and re-layouts  1.82 us (6%)
    pallas_call x1, Pallas kernels, shards(): pl.pallas_call(functools.partial(kernel, n, chunk), out_shape=jax.ShapeDt...  29.3 us
    unnamed x1, local copies, waits for them, and re-layouts  1.82 us

profile of v1, /device:TPU:24, one launch (start us, length us, event | category | flops | bytes accessed | tf_op | source)
XLA Modules:
  0.0 31.1 jit_solution(1113468623017335685)
XLA Ops:
  0.0 29.3 %shard_map.64 = bf16[128,1792]{1,0:T(8,128)(2,1)} custom-call(s32[1,128]{1,0:T(1,128)} %bitcast.1, s32[16]{0:T(128)} %lengths_ref.1, f32[2,128]{1,0:T(2,128)} %gains_ref.1, bf16[128,3584]{1,0:T(8,128)(2,1)} %hidden_hbm.1, bf16[128,1792]{1,0:T(8,128)(2,1)} %queries_hbm.1, bf16[2,3584,512]{2,1,0:T(8,128)(2,1)} %weights_hbm.1), custom_call_target="tpu_custom_call" | custom-call | tf_op jit(solution)/shard_map/pallas_call | solution.py:290
  29.3 1.8 %copy.8 = bf16[128,1792]{1,0:T(8,128)(2,1)} copy(bf16[128,1792]{1,0:T(8,128)(2,1)} %shard_map.64) | data formatting | bytes 917504

commit v2 on v1

--- a/solution.py
+++ b/solution.py
@@ -57,8 +57,13 @@
     lone = jnp.where(upper, split, split - 1)
     unused = jnp.where(upper, split - 1, split)
 
+    size = HALF // HD * rows + HALF
+
     def block(j):
-        return pl.ds(pl.multiple_of(j * rows, rows), rows)
+        return pl.ds(pl.multiple_of(j * size, size), size)
+
+    def part_of(j, at, length):
+        return pl.ds(pl.multiple_of(j * size + at, 16), length)
 
     hidden_copy = pltpu.make_async_copy(hidden_hbm, hidden, in_sem)
     hidden_copy.start()
@@ -96,23 +101,19 @@
     lane_at = lax.broadcasted_iota(jnp.int32, (rows, rows), 1)
     diagonal = row_at == lane_at
 
+    zero_lane = jnp.where(labels == 0, lane_pos, total_len)
     def to_rows(lane_values):
         spread = jnp.where(diagonal, jnp.broadcast_to(lane_values, (rows, rows)), 0)
         return jnp.sum(spread, axis=1, keepdims=True)
 
-    first = to_rows(first_lane)
-    last = to_rows(last_lane)
     label = to_rows(labels)
-    zero_lane = jnp.where(labels == 0, lane_pos, total_len)
     local_zero = jnp.min(
-        jnp.where(lane_at >= row_at, jnp.broadcast_to(zero_lane, (rows, rows)), total_len),
-        axis=1,
-        keepdims=True,
+        jnp.where(row_at >= lane_at, to_rows(zero_lane), total_len), axis=0, keepdims=True
     )
     earliest = jnp.min(zero_lane, axis=1, keepdims=True)
     zeros_at[...] = jnp.full(zeros_at.shape, total_len, jnp.int32)
     zeros_at[me] = jnp.broadcast_to(earliest, (8, rows))
-    held[block(unused), :] = jnp.zeros((rows, 2 * HALF), jnp.bfloat16)
+    held[block(unused), :] = jnp.zeros((size, HD), jnp.bfloat16)
     peak[...] = jnp.full(peak.shape, NEG, jnp.float32)
     summed[...] = jnp.zeros(summed.shape, jnp.float32)
     accum[...] = jnp.zeros(accum.shape, jnp.float32)
@@ -178,8 +179,9 @@
         key = mine[:, g * HD : (g + 1) * HD]
         square_mean = jnp.mean(key * key, axis=-1, keepdims=True)
         key = key * lax.rsqrt(square_mean + 1e-06) * gains
-        held[block(me), g * HD : (g + 1) * HD] = key.astype(jnp.bfloat16)
-    held[block(me), HALF:] = mine[:, HALF:].astype(jnp.bfloat16)
+        held[part_of(me, g * rows, rows), :] = key.astype(jnp.bfloat16)
+        value = mine[:, HALF + g * HD : HALF + (g + 1) * HD]
+        held[part_of(me, KVH * rows + g * HD, HD), :] = value.T.astype(jnp.bfloat16)
 
     def own_target(d):
         same = lax.rem(d, 2) == core
@@ -203,8 +205,7 @@
     later = jnp.min(jnp.where(device_at > me, zeros_at[...], total_len), axis=0)
     later = later[0:1, 0:1]
     zero_next = jnp.minimum(local_zero, later)
-    row_pos = offset + lax.broadcasted_iota(jnp.int32, (rows, 1), 0)
-    reach = jnp.where(label == 1, jnp.minimum(last, zero_next - 1), row_pos)
+    reach = jnp.where(labels == 1, jnp.minimum(last_lane, zero_next - 1), lane_pos)
     for copy in query_copies:
         copy.wait()
 
@@ -232,37 +233,40 @@
         def _():
             own_copy(other, me).wait_recv()
 
-        start = pl.multiple_of(chip * pair, pair)
-        key_pos = start + lax.broadcasted_iota(jnp.int32, (rows, pair), 1)
-        bias = jnp.where((key_pos >= first) & (key_pos <= reach), 0.0, NEG)
+        key_pos = chip * pair + lax.broadcasted_iota(jnp.int32, (pair, rows), 0)
+        visible = (key_pos >= first_lane) & (key_pos <= reach)
+        bias = jnp.where(visible, 0.0, NEG)
         for g in range(KVH):
-            group = pl.ds(g * GROUPS_PER * rows, GROUPS_PER * rows)
-            keys = held[pl.ds(start, pair), g * HD : (g + 1) * HD]
-            values = held[pl.ds(start, pair), HALF + g * HD : HALF + (g + 1) * HD]
-            scores = lax.dot_general(
-                query[group, :],
-                keys,
-                (((1,), (1,)), ((), ())),
-                preferred_element_type=jnp.float32,
+            keys = jnp.concatenate(
+                [held[part_of(2 * chip + i, g * rows, rows), :] for i in range(2)], axis=0
             )
-            scores = scores.reshape(GROUPS_PER, rows, pair)
-            scores = jnp.where(bias[None] == 0.0, scores, NEG)
-            scores = scores.reshape(GROUPS_PER * rows, pair)
-            old_peak = peak[group, :]
-            new_peak = jnp.maximum(old_peak, jnp.max(scores, axis=-1, keepdims=True))
-            weight = jnp.exp2((scores - new_peak) * factor_of)
-            factor = jnp.exp2((old_peak - new_peak) * factor_of)
-            peak[group, :] = new_peak
-            summed[group, :] = summed[group, :] * factor + jnp.sum(weight, axis=-1, keepdims=True)
-            mixed = jnp.dot(
-                weight.astype(jnp.bfloat16), values, preferred_element_type=jnp.float32
+            values = jnp.concatenate(
+                [held[part_of(2 * chip + i, KVH * rows + g * HD, HD), :] for i in range(2)], axis=1
             )
-            accum[group, :] = accum[group, :] * factor + mixed
+            for h in range(g * GROUPS_PER, (g + 1) * GROUPS_PER):
+                scores = lax.dot_general(
+                    keys,
+                    query[h * rows : (h + 1) * rows, :],
+                    (((1,), (1,)), ((), ())),
+                    preferred_element_type=jnp.float32,
+                )
+                scores = scores + bias
+                old_peak = peak[h : h + 1, :]
+                new_peak = jnp.maximum(old_peak, jnp.max(scores, axis=0, keepdims=True))
+                weight = jnp.exp2((scores - new_peak) * factor_of)
+                factor = jnp.exp2((old_peak - new_peak) * factor_of)
+                peak[h : h + 1, :] = new_peak
+                summed[h : h + 1, :] = summed[h : h + 1, :] * factor + jnp.sum(
+                    weight, axis=0, keepdims=True
+                )
+                mixed = jnp.dot(
+                    values, weight.astype(jnp.bfloat16), preferred_element_type=jnp.float32
+                )
+                accum[h] = accum[h] * factor + mixed
 
     for h in range(HEADS):
-        head = pl.ds(h * rows, rows)
-        result = accum[head, :] / summed[head, :]
-        out_ref[:, h * HD : (h + 1) * HD] = result.astype(out_ref.dtype)
+        result = accum[h] * (1.0 / summed[h : h + 1, :])
+        out_ref[:, h * HD : (h + 1) * HD] = result.T.astype(out_ref.dtype)
 
     @pl.loop(low, me)
     def _(d):
@@ -284,6 +288,7 @@
 
     def shards(hidden_rows, queries, labels, doc_lengths, kv_weights, key_gains):
         rows, depth = hidden_rows.shape
+        assert rows == HD
         chunk = math.gcd(depth, 512)
         any_space = pl.BlockSpec(memory_space=pl.ANY)
         vmem = pl.BlockSpec(memory_space=pltpu.VMEM)
@@ -303,11 +308,11 @@
                 pltpu.VMEM((rows, depth), jnp.bfloat16),
                 pltpu.VMEM((HEADS * rows, HD), jnp.bfloat16),
                 pltpu.VMEM(kv_weights.shape, jnp.bfloat16),
-                pltpu.VMEM((n * rows, 2 * HALF), jnp.bfloat16),
+                pltpu.VMEM((n * (KVH * rows + HALF), HD), jnp.bfloat16),
                 pltpu.VMEM((n, 8, rows), jnp.int32),
-                pltpu.VMEM((HEADS * rows, 1), jnp.float32),
-                pltpu.VMEM((HEADS * rows, 1), jnp.float32),
-                pltpu.VMEM((HEADS * rows, HD), jnp.float32),
+                pltpu.VMEM((HEADS, rows), jnp.float32),
+                pltpu.VMEM((HEADS, rows), jnp.float32),
+                pltpu.VMEM((HEADS, HD, rows), jnp.float32),
                 pltpu.SemaphoreType.DMA,
                 pltpu.SemaphoreType.DMA((HEADS,)),
                 pltpu.SemaphoreType.DMA((depth // chunk,)),

time: 31.2 us -> 25 us (0.80)
  Pallas kernels: 29.3 us -> 23 us
    pallas_call x1, Pallas kernels: 29.3 us -> 23 us  [shards(): pl.pallas_call(functools.partial(kernel, n, chunk), out_shape=jax.ShapeDt...]
where the time goes in v2:
time: 25 us; the launch traced here: 24.9 us
  Pallas kernels  23 us (92%)
  local copies, waits for them, and re-layouts  1.82 us (7%)
    pallas_call x1, Pallas kernels, shards(): pl.pallas_call(functools.partial(kernel, n, chunk), out_shape=jax.ShapeDt...  23 us
    unnamed x1, local copies, waits for them, and re-layouts  1.82 us

profile of v2, /device:TPU:24, one launch (start us, length us, event | category | flops | bytes accessed | tf_op | source)
XLA Modules:
  0.0 24.9 jit_solution(11108126829584741347)
XLA Ops:
  0.0 23.0 %shard_map.64 = bf16[128,1792]{1,0:T(8,128)(2,1)} custom-call(s32[1,128]{1,0:T(1,128)} %bitcast.1, s32[16]{0:T(128)} %lengths_ref.1, f32[2,128]{1,0:T(2,128)} %gains_ref.1, bf16[128,3584]{1,0:T(8,128)(2,1)} %hidden_hbm.1, bf16[128,1792]{1,0:T(8,128)(2,1)} %queries_hbm.1, bf16[2,3584,512]{2,1,0:T(8,128)(2,1)} %weights_hbm.1), custom_call_target="tpu_custom_call" | custom-call | tf_op jit(solution)/shard_map/pallas_call | solution.py:295
  23.0 1.8 %copy.8 = bf16[128,1792]{1,0:T(8,128)(2,1)} copy(bf16[128,1792]{1,0:T(8,128)(2,1)} %shard_map.64) | data formatting | bytes 917504

commit v3 on v2

--- a/solution.py
+++ b/solution.py
@@ -62,6 +62,11 @@
     def block(j):
         return pl.ds(pl.multiple_of(j * size, size), size)
 
+    ksize = KVH * rows
+
+    def half_of(j, half):
+        return pl.ds(pl.multiple_of(j * size + half * ksize, 16), HALF if half else ksize)
+
     def part_of(j, at, length):
         return pl.ds(pl.multiple_of(j * size + at, 16), length)
 
@@ -69,13 +74,14 @@
     hidden_copy.start()
     chunks = depth // chunk
     weight_copies = []
-    for i in range(chunks):
-        part = pl.ds(i * chunk, chunk)
-        copy = pltpu.make_async_copy(
-            weights_hbm.at[:, part, :], weights.at[:, part, :], weight_sem.at[i]
-        )
-        copy.start()
-        weight_copies.append(copy)
+    for half in range(2):
+        for i in range(chunks):
+            part = (slice(None), pl.ds(i * chunk, chunk), pl.ds(half * HALF, HALF))
+            copy = pltpu.make_async_copy(
+                weights_hbm.at[part], weights.at[part], weight_sem.at[half * chunks + i]
+            )
+            copy.start()
+            weight_copies.append(copy)
     query_copies = []
     for h in range(HEADS):
         copy = pltpu.make_async_copy(
@@ -136,52 +142,21 @@
             device_id_type=MESH,
         )
 
-    def own_copy(source, target):
+    def kv_copy(source, target, half, sem):
         return pltpu.make_async_remote_copy(
-            src_ref=held.at[block(source), :],
-            dst_ref=held.at[block(source), :],
-            send_sem=send_sem.at[target],
-            recv_sem=recv_sem.at[source],
+            src_ref=held.at[half_of(source, half), :],
+            dst_ref=held.at[half_of(source, half), :],
+            send_sem=sem,
+            recv_sem=recv_sem.at[half * n + source],
             device_id={"tok": target},
             device_id_type=MESH,
         )
 
-    def pass_copy(source):
-        return pltpu.make_async_remote_copy(
-            src_ref=held.at[block(source), :],
-            dst_ref=held.at[block(source), :],
-            send_sem=pass_sem.at[source],
-            recv_sem=recv_sem.at[source],
-            device_id={"tok": partner},
-            device_id_type=MESH,
-        )
-
-    hidden_copy.wait()
-    projected = [jnp.zeros((rows, 2 * HALF), jnp.float32) for _ in range(2)]
-    for i in range(chunks):
-        weight_copies[i].wait()
-        part = pl.ds(i * chunk, chunk)
-        for tower in range(2):
-            projected[tower] = projected[tower] + jnp.dot(
-                hidden[:, part], weights[tower, part, :], preferred_element_type=jnp.float32
-            )
-        if i == chunks // 2:
-            pl.semaphore_wait(barrier, high - low - 1)
-
-            @pl.loop(low, me)
-            def _(d):
-                zero_copy(me, d).start()
-
-    chosen = label == 1
-    gains = jnp.where(chosen, gains_ref[1:2, :], gains_ref[0:1, :])
-    mine = jnp.where(chosen, projected[1], projected[0])
-    for g in range(KVH):
-        key = mine[:, g * HD : (g + 1) * HD]
-        square_mean = jnp.mean(key * key, axis=-1, keepdims=True)
-        key = key * lax.rsqrt(square_mean + 1e-06) * gains
-        held[part_of(me, g * rows, rows), :] = key.astype(jnp.bfloat16)
-        value = mine[:, HALF + g * HD : HALF + (g + 1) * HD]
-        held[part_of(me, KVH * rows + g * HD, HD), :] = value.T.astype(jnp.bfloat16)
+    def own_copy(source, target, half):
+        return kv_copy(source, target, half, send_sem.at[half * n + target])
+
+    def pass_copy(source, half):
+        return kv_copy(source, partner, half, pass_sem.at[half * n + source])
 
     def own_target(d):
         same = lax.rem(d, 2) == core
@@ -189,13 +164,47 @@
 
     count = high - low
 
-    @pl.loop(1, count)
-    def _(k):
-        d = low + lax.rem(me - low - k + count, count)
-
-        @pl.when(own_target(d))
-        def _():
-            own_copy(me, d).start()
+    def send(half):
+        @pl.loop(1, count)
+        def _(k):
+            d = low + lax.rem(me - low - k + count, count)
+
+            @pl.when(own_target(d))
+            def _():
+                own_copy(me, d, half).start()
+
+    hidden_copy.wait()
+    chosen = label == 1
+    for half in range(2):
+        columns = pl.ds(half * HALF, HALF)
+        projected = [jnp.zeros((rows, HALF), jnp.float32) for _ in range(2)]
+        for i in range(chunks):
+            weight_copies[half * chunks + i].wait()
+            part = pl.ds(i * chunk, chunk)
+            for tower in range(2):
+                projected[tower] = projected[tower] + jnp.dot(
+                    hidden[:, part],
+                    weights[tower, part, columns],
+                    preferred_element_type=jnp.float32,
+                )
+            if half == 0 and i == chunks // 2:
+                pl.semaphore_wait(barrier, high - low - 1)
+
+                @pl.loop(low, me)
+                def _(d):
+                    zero_copy(me, d).start()
+
+        mine = jnp.where(chosen, projected[1], projected[0])
+        for g in range(KVH):
+            part = mine[:, g * HD : (g + 1) * HD]
+            if half == 0:
+                gains = jnp.where(chosen, gains_ref[1:2, :], gains_ref[0:1, :])
+                square_mean = jnp.mean(part * part, axis=-1, keepdims=True)
+                part = part * lax.rsqrt(square_mean + 1e-06) * gains
+                held[part_of(me, g * rows, rows), :] = part.astype(jnp.bfloat16)
+            else:
+                held[part_of(me, ksize + g * HD, HD), :] = part.T.astype(jnp.bfloat16)
+        send(half)
 
     @pl.loop(me + 1, high)
     def _(d):
@@ -215,23 +224,32 @@
     my_chip = me // 2
     pair = 2 * rows
 
+    def chip_at(t):
+        return chip_low + lax.rem(my_chip - chip_low + t, chip_count)
+
+    def relay(t):
+        same = 2 * chip_at(t) + core
+
+        @pl.when((t < chip_count) & (same != me) & (same >= low) & (same < high))
+        def _():
+            for half in range(2):
+                own_copy(same, me, half).wait_recv()
+
+                @pl.when(paired)
+                def _():
+                    pass_copy(same, half).start()
+
     @pl.loop(0, chip_count)
     def _(t):
-        chip = chip_low + lax.rem(my_chip - chip_low + t, chip_count)
-        same = 2 * chip + core
+        chip = chip_at(t)
         other = 2 * chip + 1 - core
-
-        @pl.when((same != me) & (same >= low) & (same < high))
-        def _():
-            own_copy(same, me).wait_recv()
-
-            @pl.when(paired)
-            def _():
-                pass_copy(same).start()
 
         @pl.when((other >= low) & (other < high))
         def _():
-            own_copy(other, me).wait_recv()
+            for half in range(2):
+                own_copy(other, me, half).wait_recv()
+
+        relay(t + 1)
 
         key_pos = chip * pair + lax.broadcasted_iota(jnp.int32, (pair, rows), 0)
         visible = (key_pos >= first_lane) & (key_pos <= reach)
@@ -274,13 +292,15 @@
 
     @pl.loop(low, high)
     def _(d):
-        @pl.when(own_target(d))
-        def _():
-            own_copy(me, d).wait_send()
-
-        @pl.when(paired & (d != me) & (lax.rem(d, 2) == core))
-        def _():
-            pass_copy(d).wait_send()
+        for half in range(2):
+
+            @pl.when(own_target(d))
+            def _():
+                own_copy(me, d, half).wait_send()
+
+            @pl.when(paired & (d != me) & (lax.rem(d, 2) == core))
+            def _():
+                pass_copy(d, half).wait_send()
 
 
 def solution(mesh):
@@ -315,10 +335,10 @@
                 pltpu.VMEM((HEADS, HD, rows), jnp.float32),
                 pltpu.SemaphoreType.DMA,
                 pltpu.SemaphoreType.DMA((HEADS,)),
-                pltpu.SemaphoreType.DMA((depth // chunk,)),
-                pltpu.SemaphoreType.DMA((n,)),
-                pltpu.SemaphoreType.DMA((n,)),
-                pltpu.SemaphoreType.DMA((n,)),
+                pltpu.SemaphoreType.DMA((2 * depth // chunk,)),
+                pltpu.SemaphoreType.DMA((2 * n,)),
+                pltpu.SemaphoreType.DMA((2 * n,)),
+                pltpu.SemaphoreType.DMA((2 * n,)),
                 pltpu.SemaphoreType.DMA((n,)),
                 pltpu.SemaphoreType.DMA((n,)),
             ],

time: 25 us -> 23 us (0.920)
  the two profiles are of different devices: /device:TPU:24 before, /device:TPU:14 now
where the time goes in v3:
time: 23 us; the launch traced here: 22.9 us
  Pallas kernels  21.1 us (92%)
  local copies, waits for them, and re-layouts  1.82 us (8%)
    pallas_call x1, Pallas kernels, shards(): pl.pallas_call(functools.partial(kernel, n, chunk), out_shape=jax.ShapeDt...  21.1 us
    unnamed x1, local copies, waits for them, and re-layouts  1.82 us

profile of v3, /device:TPU:14, one launch (start us, length us, event | category | flops | bytes accessed | tf_op | source)
XLA Modules:
  0.0 22.9 jit_solution(4324810795191810370)
XLA Ops:
  0.0 21.1 %shard_map.64 = bf16[128,1792]{1,0:T(8,128)(2,1)} custom-call(s32[1,128]{1,0:T(1,128)} %bitcast.1, s32[16]{0:T(128)} %lengths_ref.1, f32[2,128]{1,0:T(2,128)} %gains_ref.1, bf16[128,3584]{1,0:T(8,128)(2,1)} %hidden_hbm.1, bf16[128,1792]{1,0:T(8,128)(2,1)} %queries_hbm.1, bf16[2,3584,512]{2,1,0:T(8,128)(2,1)} %weights_hbm.1), custom_call_target="tpu_custom_call" | custom-call | tf_op jit(solution)/shard_map/pallas_call | solution.py:315
  21.1 1.8 %copy.8 = bf16[128,1792]{1,0:T(8,128)(2,1)} copy(bf16[128,1792]{1,0:T(8,128)(2,1)} %shard_map.64) | data formatting | bytes 917504
